TPU v7x, 32 devices: a whole 2x2x4 slice. The times are simulated.
32 devices in a mesh: groups: 2 (over y), span: 4 (over z), mp: 2 (over x), seq: 2 (over core).
Axes of the slice: x: 2, y: 2, z: 4, core: 2. Of those that a mesh axis runs over, the one named last changes fastest.
Arguments:
- query: bfloat16 [4, 8, 144, 3072], P(None, ('groups', 'span'), None, ('mp', 'seq')), parts along dimension 1, may hold values from -600 to 600
- noisy_kv: bfloat16 [4, 2, 8, 144, 3072], P(None, None, ('groups', 'span'), None, ('mp', 'seq')), parts along dimension 2, may hold values from -11 to 11
- clean_kv: bfloat16 [2, 8, 144, 3072], P(None, ('groups', 'span'), None, ('mp', 'seq')), parts along dimension 1, may hold values from -11 to 11
- causal_mask: int32 [8, 4], P('groups'), parts along dimension 0, may hold values from 0 to 1, as said below
- step_index: int32 [8, 4], P('groups'), parts along dimension 0, may hold values from 0 to 63, as said below
- finished: bfloat16 [8, 144, 3072], P(('groups', 'span'), None, ('mp', 'seq')), parts along dimension 0, may hold values from -6 to 6
- w_in: bfloat16 [3072, 512], P(('mp', 'seq')), may hold values from -0.109375 to 0.109375
- conv_w: bfloat16 [3, 512, 512], replicated, may hold values from -0.15625 to 0.15625
- fade_count: int32 [8], P(('groups', 'span')), parts along dimension 0, may hold values from 0 to 2, as said below
Outputs:
- attended: bfloat16 [4, 8, 144, 3072], P(None, ('groups', 'span'), None, ('mp', 'seq')), parts along dimension 1
- decoded: bfloat16 [8, 144, 512], P(('groups', 'span'), ('mp', 'seq')), parts along dimension 0
There are 2 independent parts, one for each index of `groups`. A program takes and returns all parts, laid end to end along the dimension named above; an argument that names none is the same for every part. Nothing has to cross between parts.
Inputs may be any that keep to these rules, and one draw needn't show every extreme that they name: `causal_mask`: zero on and above the diagonal. `step_index`: each row counts up by one from its first entry; some row starts at 0 and some at 60. `fade_count`: some segment other than the first has 2.
All inputs are finite; a program needn't handle non-finite values.
Results may differ from a plain program's by a relative error of at most 0.015.
Values may be sent and summed in bfloat16 or wider, within the bound.
A program may use at most 64 MiB of HBM per device.

v0:
```python
import functools
import math

import jax
import jax.numpy as jnp
from jax import lax
from jax.experimental import pallas as pl
from jax.experimental.pallas import tpu as pltpu
from jax.sharding import PartitionSpec as P

FR = 6
HEADS = 24
HD = 128
KT = 3
FADE = 2
NSTEPS = 64
MESH = pl.DeviceIdType.MESH
LOG2E = 1.4426950408889634
F32 = jnp.float32
BF16 = jnp.bfloat16


def nt_dot(a, b):
    return lax.dot_general(a, b, (((1,), (1,)), ((), ())), preferred_element_type=F32)


def tn_dot(a, b):
    return lax.dot_general(a, b, (((0,), (0,)), ((), ())), preferred_element_type=F32)


def kernel(
    dims,
    mask_hbm, index_hbm, fade_hbm, query_hbm, noisy_hbm, clean_hbm, fin_hbm, win_hbm, conv_hbm,
    att_ref, dec_ref,
    q_ref, noisy_ref, fin_ref, win_ref, conv_ref, own_ref, kv_ref,
    m_ref, l_ref, o_ref, part_ref, part_in, hid_ref, prev_ref, stat_ref, stat_in,
    mask_ref, index_ref, fade_ref,
    load_sem, own_sem, kv_send, kv_recv, part_send, part_recv, hid_send, hid_recv, stat_send, stat_recv,
):
    n, mp_n, seq_n, steps, ct, heads, rows, rp = dims
    group = mp_n * seq_n
    p = lax.axis_index("span")
    g = lax.axis_index("mp") * seq_n + lax.axis_index("seq")
    total = steps * ct

    def peer(d):
        other = lax.rem(g + d, group)
        return other, {"mp": other // seq_n, "seq": lax.rem(other, seq_n)}

    own_loads = []
    for h in range(heads):
        copy = pltpu.make_async_copy(
            clean_hbm.at[:, 0, :, pl.ds(h * HD, HD)], own_ref.at[h], own_sem.at[h]
        )
        copy.start()
        own_loads.append(copy)
    barrier = pltpu.get_barrier_semaphore()

    @pl.when(p > 0)
    def _():
        pl.semaphore_signal(barrier, inc=1, device_id={"span": p - 1}, device_id_type=MESH)

    @pl.when(p < n - 1)
    def _():
        pl.semaphore_signal(barrier, inc=1, device_id={"span": p + 1}, device_id_type=MESH)

    for d in range(1, group):
        pl.semaphore_signal(barrier, inc=1, device_id=peer(d)[1], device_id_type=MESH)

    ends = (p > 0).astype(jnp.int32) + (p < n - 1).astype(jnp.int32)
    pl.semaphore_wait(barrier, group - 1 + ends)

    def kv_copy(src, slot, h):
        return pltpu.make_async_remote_copy(
            src_ref=src, dst_ref=kv_ref.at[slot, h], send_sem=kv_send.at[slot, h],
            recv_sem=kv_recv.at[slot, h], device_id={"span": p + 1}, device_id_type=MESH,
        )

    for h in range(heads):
        own_loads[h].wait()

        @pl.when(p < n - 1)
        def _():
            kv_copy(own_ref.at[h], 0, h).start()

    loads = []
    for i, (src, dst) in enumerate(
        (
            (fin_hbm, fin_ref), (win_hbm, win_ref), (query_hbm, q_ref), (noisy_hbm, noisy_ref),
            (conv_hbm, conv_ref), (mask_hbm, mask_ref), (index_hbm, index_ref), (fade_hbm, fade_ref),
        )
    ):
        copy = pltpu.make_async_copy(src, dst, load_sem.at[i])
        copy.start()
        loads.append(copy)

    loads[0].wait()
    loads[1].wait()
    partial = jnp.dot(fin_ref[0], win_ref[...], preferred_element_type=F32).astype(BF16)
    row = lax.broadcasted_iota(jnp.int32, (rp, ct), 0)
    col = lax.broadcasted_iota(jnp.int32, (rp, ct), 1)
    for o in range(group):
        pick = jnp.where((row < rows) & (col == row + o * rows), 1.0, 0.0).astype(BF16)
        part_ref[o] = jnp.dot(pick, partial, preferred_element_type=F32).astype(BF16)

    for i in (2, 3, 5, 6, 7):
        loads[i].wait()
    lane = lax.broadcasted_iota(jnp.int32, (1, total), 1)
    indices = jnp.zeros((1, total), F32)
    for s in range(steps):
        value = index_ref[p, s].astype(F32)
        indices = jnp.where((lane >= s * ct) & (lane < (s + 1) * ct), value, indices)
    fraction = 1.0 - indices / NSTEPS
    level = 3.0 * fraction / (1.0 + 2.0 * fraction)
    scale = (0.5 + level) * (LOG2E / math.sqrt(HD))

    def own_head(h):
        cols = slice(h * HD, (h + 1) * HD)
        ms, ls, os = [], [], []
        for s in range(steps):
            step_index = jnp.full((1, ct), index_ref[p, s].astype(F32), F32)
            part = 1.0 - step_index / NSTEPS
            own_scale = (0.5 + 3.0 * part / (1.0 + 2.0 * part)) * (LOG2E / math.sqrt(HD))
            scores = nt_dot(noisy_ref[s, 0, 0, :, cols], q_ref[s, 0, :, cols]) * own_scale
            m = scores.max(0, keepdims=True)
            w = jnp.exp2(scores - m)
            ms.append(m)
            ls.append(w.sum(0, keepdims=True))
            os.append(tn_dot(noisy_ref[s, 1, 0, :, cols], w.astype(BF16)))
        m_ref[h] = jnp.concatenate(ms, 1)
        l_ref[h] = jnp.concatenate(ls, 1)
        o_ref[h] = jnp.concatenate(os, 1)

    def part_copy(d):
        other, where = peer(d)
        return pltpu.make_async_remote_copy(
            src_ref=part_ref.at[other], dst_ref=part_in.at[d - 1], send_sem=part_send.at[d - 1],
            recv_sem=part_recv.at[d - 1], device_id=where, device_id_type=MESH,
        )

    hid_copy = pltpu.make_async_remote_copy(
        src_ref=hid_ref, dst_ref=prev_ref, send_sem=hid_send, recv_sem=hid_recv,
        device_id={"span": p + 1}, device_id_type=MESH,
    )

    for h in range(heads):
        own_head(h)
        if h == 0:
            for d in range(1, group):
                part_copy(d).start()
        if h == heads // 2:
            for d in range(1, group):
                part_copy(d).wait()
            summed = part_ref[g].astype(F32)
            for d in range(1, group):
                summed = summed + part_in[d - 1].astype(F32)
            hid_ref[...] = summed.astype(BF16)
    loads[4].wait()

    @pl.when(p < n - 1)
    def _():
        hid_copy.start()

    def absorb(j, h):
        cols = slice(h * HD, (h + 1) * HD)
        queries = q_ref[:, 0, :, cols].reshape(total, HD)
        visible = mask_ref[p, p - 1 - j]
        bias = jnp.where(visible > 0, 0.0, -1e30).astype(F32)
        scores = nt_dot(kv_ref[j, h, 0], queries) * scale + bias
        old = m_ref[h]
        m = jnp.maximum(old, scores.max(0, keepdims=True))
        factor = jnp.exp2(old - m)
        w = jnp.exp2(scores - m)
        m_ref[h] = m
        l_ref[h] = l_ref[h] * factor + w.sum(0, keepdims=True)
        o_ref[h] = o_ref[h] * factor + tn_dot(kv_ref[j, h, 1], w.astype(BF16))

    def block(j, carry):
        for h in range(heads):
            kv_copy(own_ref.at[h], j, h).wait_recv()

            @pl.when(p < n - 1)
            def _():
                kv_copy(kv_ref.at[j, h], j + 1, h).start()

            absorb(j, h)
        return carry

    def decode():
        @pl.when(p > 0)
        def _():
            hid_copy.wait_recv()

        @pl.when(p == 0)
        def _():
            prev_ref[...] = jnp.zeros_like(prev_ref)

        now = hid_ref[...].astype(F32)
        before = prev_ref[...].astype(F32)
        width = now.shape[1]
        frame = lax.rem(lax.broadcasted_iota(jnp.int32, (rp, width), 0), FR)
        mixed = jnp.zeros((2 * rp, width), F32)
        for k in range(KT):
            late = pltpu.roll(before, k, 0) if k else before
            if k:
                cur = jnp.where(
                    frame >= k, pltpu.roll(now, k, 0), pltpu.roll(before, rp + k - FR, 0)
                )
            else:
                cur = now
            window = jnp.concatenate([cur, late], 0).astype(BF16)
            mixed = mixed + jnp.dot(window, conv_ref[k], preferred_element_type=F32)
        frames = jax.nn.silu(mixed).astype(BF16).astype(F32)
        cur, late = frames[:rp], frames[rp:]
        fade = fade_ref[0]
        aligned = jnp.zeros_like(late)
        for count in range(1, FADE + 1):
            aligned = jnp.where(fade == count, pltpu.roll(late, rp - FR + count, 0), aligned)
        active = (frame < fade) & (p > 0)
        fade_f = fade.astype(F32)
        weight = (frame.astype(F32) + 1.0) / (jnp.zeros((rp, width), F32) + fade_f + 1.0)
        mix = weight * cur + (1.0 - weight) * aligned
        dec_ref[0] = jnp.where(active, mix, cur)[:rows].astype(BF16)

    first = jnp.minimum(p, 1)
    lax.fori_loop(0, first, block, 0)
    decode()
    lax.fori_loop(first, p, block, 0)

    squares = jnp.zeros((1, total), F32)
    for h in range(heads):
        averaged = o_ref[h] / l_ref[h]
        o_ref[h] = averaged
        squares = squares + jnp.sum(averaged * averaged, 0, keepdims=True)
    stat_ref[...] = squares

    def stat_copy(d):
        return pltpu.make_async_remote_copy(
            src_ref=stat_ref, dst_ref=stat_in.at[d - 1], send_sem=stat_send.at[d - 1],
            recv_sem=stat_recv.at[d - 1], device_id=peer(d)[1], device_id_type=MESH,
        )

    for d in range(1, group):
        stat_copy(d).start()
    for d in range(1, group):
        stat_copy(d).wait()
    for d in range(1, group):
        squares = squares + stat_in[d - 1]
    inverse = lax.rsqrt(squares / (HD * heads * group) + 1e-06)
    for h in range(heads):
        normed = jnp.transpose(o_ref[h] * inverse).astype(BF16)
        for s in range(steps):
            att_ref[s, 0, :, h * HD : (h + 1) * HD] = normed[s * ct : (s + 1) * ct]

    @pl.when(p < n - 1)
    def _():
        hid_copy.wait_send()

        def drain(j, carry):
            for h in range(heads):
                kv_copy(own_ref.at[h], j, h).wait_send()
            return carry

        lax.fori_loop(0, p + 1, drain, 0)


def per_device(sizes, query, noisy_kv, clean_kv, causal_mask, step_index, finished, w_in, conv_w, fade_count):
    n, mp_n, seq_n = sizes
    group = mp_n * seq_n
    steps, _, ct, width = query.shape
    heads = width // HD
    channels = w_in.shape[1]
    rows = ct // group
    rp = -(-rows // 16) * 16
    total = steps * ct
    dims = (n, mp_n, seq_n, steps, ct, heads, rows, rp)
    vmem = pltpu.VMEM
    dma = pltpu.SemaphoreType.DMA
    hbm = pl.BlockSpec(memory_space=pltpu.HBM)
    out = pl.BlockSpec(memory_space=pltpu.VMEM)
    slots = max(n - 1, 1)
    return pl.pallas_call(
        functools.partial(kernel, dims),
        out_shape=(
            jax.ShapeDtypeStruct(query.shape, BF16),
            jax.ShapeDtypeStruct((1, rows, channels), BF16),
        ),
        in_specs=[hbm] * 9,
        out_specs=(out, out),
        scratch_shapes=[
            vmem(query.shape, BF16),
            vmem(noisy_kv.shape, BF16),
            vmem(finished.shape, BF16),
            vmem(w_in.shape, BF16),
            vmem(conv_w.shape, BF16),
            vmem((heads, 2, ct, HD), BF16),
            vmem((slots, heads, 2, ct, HD), BF16),
            vmem((heads, 1, total), F32),
            vmem((heads, 1, total), F32),
            vmem((heads, HD, total), F32),
            vmem((group, rp, channels), BF16),
            vmem((group - 1, rp, channels), BF16),
            vmem((rp, channels), BF16),
            vmem((rp, channels), BF16),
            vmem((1, total), F32),
            vmem((group - 1, 1, total), F32),
            pltpu.SMEM(causal_mask.shape, jnp.int32),
            pltpu.SMEM(step_index.shape, jnp.int32),
            pltpu.SMEM(fade_count.shape, jnp.int32),
            dma((8,)),
            dma((heads,)),
            dma((slots, heads)),
            dma((slots, heads)),
            dma((group - 1,)),
            dma((group - 1,)),
            dma,
            dma,
            dma((group - 1,)),
            dma((group - 1,)),
        ],
        compiler_params=pltpu.CompilerParams(
            collective_id=0, has_side_effects=True, vmem_limit_bytes=67043328
        ),
    )(causal_mask, step_index, fade_count, query, noisy_kv, clean_kv, finished, w_in, conv_w)


def solution(mesh):
    placed = (
        P(None, ("groups", "span"), None, ("mp", "seq")),
        P(None, None, ("groups", "span"), None, ("mp", "seq")),
        P(None, ("groups", "span"), None, ("mp", "seq")),
        P("groups", None),
        P("groups", None),
        P(("groups", "span"), None, ("mp", "seq")),
        P(("mp", "seq"), None),
        P(),
        P(("groups", "span")),
    )
    sizes = (mesh.shape["span"], mesh.shape["mp"], mesh.shape["seq"])
    return jax.shard_map(
        functools.partial(per_device, sizes),
        mesh=mesh,
        in_specs=placed,
        out_specs=(
            P(None, ("groups", "span"), None, ("mp", "seq")),
            P(("groups", "span"), ("mp", "seq"), None),
        ),
        check_vma=False,
    )
```

profile of v0, /device:TPU:29, one launch (start us, length us, event | category | flops | bytes accessed | tf_op | source)
XLA Modules:
  0.0 42.0 jit_solution(3847761856411983248)
XLA Ops:
  1.3 37.9 %shard_map.104 = (bf16[4,1,144,768]{3,2,1,0:T(8,128)(2,1)}, bf16[1,36,512]{2,1,0:T(8,128)(2,1)}) custom-call(s32[4,4]{1,0:T(4,128)} %mask_hbm.1, s32[4,4]{1,0:T(4,128)} %index_hbm.1, s32[1]{0:T(128)S(6)} %copy.13.fade_hbm, bf16[4,1,144,768]{3,2,1,0:T(8,128)(2,1)} %query_hbm.1, bf16[4,2,1,144,768]{4,3,2,1,0:T(8,128)(2,1)} %noisy_hbm.1, ...), custom_call_target="tpu_custom_call" | custom-call | tf_op jit(solution)/shard_map/pallas_call | solution.py:282
  39.2 0.0 copy-start
  39.2 2.1 %copy.14 = bf16[4,1,144,768]{3,2,1,0:T(8,128)(2,1)} copy(bf16[4,1,144,768]{3,2,1,0:T(8,128)(2,1)} %get-tuple-element.4) | data formatting | bytes 1769472
  41.3 0.0 copy-done
  41.3 0.6 %copy.15 = bf16[1,36,512]{2,1,0:T(8,128)(2,1)} copy(bf16[1,36,512]{2,1,0:T(8,128)(2,1)S(1)} %copy-done) | data formatting | bytes 73728
Async XLA Ops:
  39.2 2.2 %copy-start = (bf16[1,36,512]{2,1,0:T(8,128)(2,1)S(1)}, bf16[1,36,512]{2,1,0:T(8,128)(2,1)}, u32[]{:S(2)}) copy-start(bf16[1,36,512]{2,1,0:T(8,128)(2,1)} %get-tuple-element.5) | copy-start | bytes 110596
where the time goes:
time: 42.1 us; the launch traced here: 42 us
  Pallas kernels  37.9 us (90%)
  local copies, waits for them, and re-layouts  2.77 us (7%)
  between operations  1.3 us (3%)
    pallas_call x1, Pallas kernels, per_device(): pl.pallas_call(functools.partial(kernel, dims), out_shape=(jax.ShapeDtype...  37.9 us
    unnamed x4, local copies, waits for them, and re-layouts  2.77 us

commit v1 on v0

--- a/solution.py
+++ b/solution.py
@@ -264,6 +264,17 @@
         lax.fori_loop(0, p + 1, drain, 0)
 
 
+def write_out(att_ref, dec_ref, att_hbm, dec_hbm, sem):
+    copies = [
+        pltpu.make_async_copy(att_ref, att_hbm, sem.at[0]),
+        pltpu.make_async_copy(dec_ref, dec_hbm, sem.at[1]),
+    ]
+    for copy in copies:
+        copy.start()
+    for copy in copies:
+        copy.wait()
+
+
 def per_device(sizes, query, noisy_kv, clean_kv, causal_mask, step_index, finished, w_in, conv_w, fade_count):
     n, mp_n, seq_n = sizes
     group = mp_n * seq_n
@@ -279,7 +290,12 @@
     hbm = pl.BlockSpec(memory_space=pltpu.HBM)
     out = pl.BlockSpec(memory_space=pltpu.VMEM)
     slots = max(n - 1, 1)
-    return pl.pallas_call(
+    arguments = [
+        pltpu.with_memory_space_constraint(x, pltpu.HBM)
+        for x in (causal_mask, step_index, query, noisy_kv, clean_kv, finished, w_in, conv_w)
+    ]
+    arguments.insert(2, fade_count)
+    attended, decoded = pl.pallas_call(
         functools.partial(kernel, dims),
         out_shape=(
             jax.ShapeDtypeStruct(query.shape, BF16),
@@ -319,9 +335,20 @@
             dma((group - 1,)),
         ],
         compiler_params=pltpu.CompilerParams(
-            collective_id=0, has_side_effects=True, vmem_limit_bytes=67043328
+            collective_id=0, has_side_effects=True, vmem_limit_bytes=28 * 2**20
         ),
-    )(causal_mask, step_index, fade_count, query, noisy_kv, clean_kv, finished, w_in, conv_w)
+    )(*arguments)
+    return pl.pallas_call(
+        write_out,
+        out_shape=(
+            jax.ShapeDtypeStruct(attended.shape, BF16),
+            jax.ShapeDtypeStruct(decoded.shape, BF16),
+        ),
+        in_specs=[out, out],
+        out_specs=(hbm, hbm),
+        scratch_shapes=[dma((2,))],
+        compiler_params=pltpu.CompilerParams(vmem_limit_bytes=4 * 2**20),
+    )(attended, decoded)
 
 
 def solution(mesh):

time: 42.1 us -> 39.3 us (0.933)
  local copies, waits for them, and re-layouts: 2.77 us -> 0 us
    unnamed x4 -> x0, local copies, waits for them, and re-layouts: 2.77 us -> none
    pallas_call x0 -> x1, Pallas kernels: none -> 0.93 us  [per_device(): pl.pallas_call(write_out, out_shape=(jax.ShapeDtypeStruct(attended.shape,...]
    pallas_call x1, Pallas kernels: 37.9 us -> 37 us  [per_device(): pl.pallas_call(functools.partial(kernel, dims), out_shape=(jax.ShapeDtype...]
where the time goes in v1:
time: 39.3 us; the launch traced here: 39.2 us
  Pallas kernels  37.9 us (96%)
  between operations  1.29 us (3%)
    pallas_call x1, Pallas kernels, per_device(): pl.pallas_call(functools.partial(kernel, dims), out_shape=(jax.ShapeDtype...  37 us
    pallas_call x1, Pallas kernels, per_device(): pl.pallas_call(write_out, out_shape=(jax.ShapeDtypeStruct(attended.shape,...  0.93 us

profile of v1, /device:TPU:29, one launch (start us, length us, event | category | flops | bytes accessed | tf_op | source)
XLA Modules:
  0.0 39.2 jit_solution(2490225638393932029)
XLA Ops:
  1.3 37.0 %shard_map.104 = (bf16[4,1,144,768]{3,2,1,0:T(8,128)(2,1)S(1)}, bf16[1,36,512]{2,1,0:T(8,128)(2,1)S(1)}) custom-call(s32[4,4]{1,0:T(4,128)} %mask_hbm.1, s32[4,4]{1,0:T(4,128)} %index_hbm.1, s32[1]{0:T(128)S(6)} %copy.11.fade_hbm, bf16[4,1,144,768]{3,2,1,0:T(8,128)(2,1)} %query_hbm.1, bf16[4,2,1,144,768]{4,3,2,1,0:T(8,128)(2,1)} %noisy_hbm.1, ...), custom_call_target="tpu_custom_call" | custom-call | tf_op jit(solution)/shard_map/pallas_call | solution.py:298
  38.3 0.9 %shard_map.105 = (bf16[4,1,144,768]{3,2,1,0:T(8,128)(2,1)}, bf16[1,36,512]{2,1,0:T(8,128)(2,1)}) custom-call(bf16[4,1,144,768]{3,2,1,0:T(8,128)(2,1)S(1)} %get-tuple-element.4.att_ref, bf16[1,36,512]{2,1,0:T(8,128)(2,1)S(1)} %get-tuple-element.5.dec_ref), custom_call_target="tpu_custom_call" | custom-call | tf_op jit(solution)/shard_map/pallas_call | solution.py:341

commit v2 on v1

v2 whole, which is shorter than its diff:
```python
import functools
import math

import jax
import jax.numpy as jnp
from jax import lax
from jax.experimental import pallas as pl
from jax.experimental.pallas import tpu as pltpu
from jax.sharding import PartitionSpec as P

FR = 6
HD = 128
KT = 3
FADE = 2
NSTEPS = 64
LANES = 128
MESH = pl.DeviceIdType.MESH
LOG2E = 1.4426950408889634
LOW = -1e30
F32 = jnp.float32
BF16 = jnp.bfloat16


def nt_dot(a, b):
    return lax.dot_general(a, b, (((1,), (1,)), ((), ())), preferred_element_type=F32)


def tn_dot(a, b):
    return lax.dot_general(a, b, (((0,), (0,)), ((), ())), preferred_element_type=F32)


def head_cols(h):
    return pl.ds(pl.multiple_of(h * HD, HD), HD)


def kernel(
    dims,
    mask_hbm, index_hbm, fade_hbm, query_hbm, noisy_hbm, clean_hbm, fin_hbm, win_hbm, conv_hbm,
    avg_ref, inv_ref, dec_ref,
    q_ref, noisy_ref, fin_ref, win_ref, conv_ref, own_ref, kv_ref, lastq_ref,
    m_ref, l_ref, o_ref, osend_ref, oin_ref, mlsend_ref, mlin_ref,
    part_ref, part_in, hid_ref, prev_ref, sq_ref, stat_in, mask_ref, index_ref, fade_ref,
    load_sem, kv_send, kv_recv, lastq_send, lastq_recv, o_send, o_recv, ml_send, ml_recv,
    part_send, part_recv, hid_send, hid_recv, stat_send, stat_recv,
):
    n, mp_n, seq_n, steps, ct, heads, rows, rp, main = dims
    group = mp_n * seq_n
    rest = ct - main
    total = steps * ct
    p = lax.axis_index("span")
    g = lax.axis_index("mp") * seq_n + lax.axis_index("seq")
    last, helper = n - 1, n - 2
    feeds = p < helper
    helps = p == helper
    ends = (p == last) & (n > 1)
    blocks = max(helper, 0)
    routed = min(2, heads) if n > 1 else 0

    def peer(d):
        other = lax.rem(g + d, group)
        return other, {"mp": other // seq_n, "seq": lax.rem(other, seq_n)}

    barrier = pltpu.get_barrier_semaphore()

    @pl.when(p > 0)
    def _():
        pl.semaphore_signal(barrier, inc=1, device_id={"span": p - 1}, device_id_type=MESH)

    @pl.when(p < n - 1)
    def _():
        pl.semaphore_signal(barrier, inc=1, device_id={"span": p + 1}, device_id_type=MESH)

    for d in range(1, group):
        pl.semaphore_signal(barrier, inc=1, device_id=peer(d)[1], device_id_type=MESH)

    near = (p > 0).astype(jnp.int32) + (p < n - 1).astype(jnp.int32)
    loads = []
    for i, (src, dst) in enumerate(
        (
            (fin_hbm, fin_ref), (win_hbm, win_ref), (query_hbm, q_ref), (noisy_hbm, noisy_ref),
            (mask_hbm, mask_ref), (index_hbm, index_ref), (fade_hbm, fade_ref), (conv_hbm, conv_ref),
            (clean_hbm, own_ref),
        )
    ):
        loads.append(pltpu.make_async_copy(src, dst, load_sem.at[i]))
    for copy in loads[:2]:
        copy.start()

    pl.semaphore_wait(barrier, group - 1 + near)

    def kv_copy(src, slot, h):
        return pltpu.make_async_remote_copy(
            src_ref=src, dst_ref=kv_ref.at[slot, h], send_sem=kv_send.at[slot, h],
            recv_sem=kv_recv.at[slot, h], device_id={"span": p + 1}, device_id_type=MESH,
        )

    def own_kv_copy(h):
        return kv_copy(clean_hbm.at[:, 0, :, head_cols(h)], 0, h)

    def lastq_copy(h):
        return pltpu.make_async_remote_copy(
            src_ref=query_hbm.at[:, 0, :, head_cols(h)], dst_ref=lastq_ref.at[h],
            send_sem=lastq_send.at[h], recv_sem=lastq_recv.at[h],
            device_id={"span": p - 1}, device_id_type=MESH,
        )

    def o_copy(h):
        return pltpu.make_async_remote_copy(
            src_ref=osend_ref.at[h], dst_ref=oin_ref.at[h], send_sem=o_send.at[h],
            recv_sem=o_recv.at[h], device_id={"span": p + 1}, device_id_type=MESH,
        )

    def ml_copy(h):
        return pltpu.make_async_remote_copy(
            src_ref=mlsend_ref.at[h], dst_ref=mlin_ref.at[h], send_sem=ml_send.at[h],
            recv_sem=ml_recv.at[h], device_id={"span": p + 1}, device_id_type=MESH,
        )

    def part_copy(d):
        other, where = peer(d)
        return pltpu.make_async_remote_copy(
            src_ref=part_ref.at[other], dst_ref=part_in.at[d - 1], send_sem=part_send.at[d - 1],
            recv_sem=part_recv.at[d - 1], device_id=where, device_id_type=MESH,
        )

    def stat_copy(d):
        return pltpu.make_async_remote_copy(
            src_ref=sq_ref, dst_ref=stat_in.at[d - 1], send_sem=stat_send.at[d - 1],
            recv_sem=stat_recv.at[d - 1], device_id=peer(d)[1], device_id_type=MESH,
        )

    hid_copy = pltpu.make_async_remote_copy(
        src_ref=hid_ref, dst_ref=prev_ref, send_sem=hid_send, recv_sem=hid_recv,
        device_id={"span": p + 1}, device_id_type=MESH,
    )

    def every_head(body, first=0):
        lax.fori_loop(first, heads, lambda h, c: (body(h), c)[1], 0)

    ahead = max(routed, 1)

    @pl.when(feeds)
    def _():
        for h in range(ahead):
            own_kv_copy(h).start()

    @pl.when(helps)
    def _():
        for h in range(routed):
            own_kv_copy(h).start()

    @pl.when(ends)
    def _():
        every_head(lambda h: lastq_copy(h).start(), routed)

    for copy in loads[2:8]:
        copy.start()

    @pl.when(helps)
    def _():
        loads[8].start()

    def arrive(j, h):
        kv_copy(kv_ref.at[j, h], j, h).wait_recv()

    def hand_on(j, h):
        arrive(j, h)
        kv_copy(kv_ref.at[j, h], j + 1, h).start()

    def pass_on(h):
        lax.fori_loop(0, p, lambda j, c: (hand_on(j, h), c)[1], 0)

        @pl.when((h + 1 >= ahead) & (h + 1 < heads))
        def _():
            own_kv_copy(h + 1).start()

    @pl.when(feeds)
    def _():
        for h in range(ahead):
            pass_on(h)

    loads[0].wait()
    loads[1].wait()
    partial = jnp.dot(fin_ref[0], win_ref[...], preferred_element_type=F32).astype(BF16)
    row = lax.broadcasted_iota(jnp.int32, (rp, ct), 0)
    col = lax.broadcasted_iota(jnp.int32, (rp, ct), 1)
    for o in range(group):
        pick = jnp.where((row < rows) & (col == row + o * rows), 1.0, 0.0).astype(BF16)
        part_ref[o] = jnp.dot(pick, partial, preferred_element_type=F32).astype(BF16)
    for d in range(1, group):
        part_copy(d).start()

    for i in (2, 3, 4, 5, 6):
        loads[i].wait()

    @pl.when(helps)
    def _():
        loads[8].wait()

    lane = lax.broadcasted_iota(jnp.int32, (1, total), 1)
    split = steps * main
    step_of = jnp.zeros((1, total), jnp.int32)
    for s in range(1, steps):
        step_of = step_of + (
            ((lane >= s * main) & (lane < split)) | (lane >= split + s * rest)
        ).astype(jnp.int32)

    def scale_row(segment):
        indices = jnp.zeros((1, total), F32)
        for s in range(steps):
            indices = jnp.where(step_of == s, index_ref[segment, s].astype(F32), indices)
        fraction = 1.0 - indices / NSTEPS
        level = 3.0 * fraction / (1.0 + 2.0 * fraction)
        return (0.5 + level) * (LOG2E / math.sqrt(HD))

    scale = scale_row(p)
    last_scale = scale_row(last)

    wide = 4
    tiles = []
    for s in range(0, steps if main else 0, wide):
        held = range(s, min(s + wide, steps))
        tiles.append((s * main, len(held) * main, [(k, 0, main) for k in held]))
    if rest:
        tiles.append((split, steps * rest, [(s, main, ct) for s in range(steps)]))

    def query_tile(t, row):
        return jnp.concatenate([row(*piece) for piece in tiles[t][2]], 0)

    def own_query(h):
        return lambda s, lo, hi: q_ref[s, 0, lo:hi, head_cols(h)]

    def last_query(h):
        return lambda s, lo, hi: lastq_ref[h, s, lo:hi, :]

    def part_of(ref, tile):
        return ref[:, tile[0] : tile[0] + tile[1]]

    def one_pass(c, scored, old=None):
        tops = []
        for scores, _, visible in scored:
            top = scores.max(0, keepdims=True) * c
            tops.append(top if visible is None else jnp.where(visible > 0, top, LOW))
        m = functools.reduce(jnp.maximum, tops)
        if old is not None:
            m = jnp.maximum(m, old[0])
        l, o = 0.0, 0.0
        for scores, values, visible in scored:
            base = m if visible is None else jnp.where(visible > 0, m, -LOW)
            w = jnp.exp2(scores * c - base)
            l = l + w.sum(0, keepdims=True)
            o = o + values(w)
        if old is not None:
            factor = jnp.exp2(old[0] - m)
            l = l + old[1] * factor
            o = o + old[2] * factor
        return m, l, o

    def plain(keys, values, queries, visible):
        return nt_dot(keys, queries), lambda w: tn_dot(values, w.astype(BF16)), visible

    def noisy(h, t, queries):
        keys = lambda s: noisy_ref[s, 0, 0, :, head_cols(h)]
        values = lambda s: noisy_ref[s, 1, 0, :, head_cols(h)]
        if tiles[t][0] < split:
            pieces = [k for k, _, _ in tiles[t][2]]
            cut = lambda x, i: x[:, i * main : (i + 1) * main]
            scores = jnp.concatenate(
                [nt_dot(keys(k), queries[i * main : (i + 1) * main]) for i, k in enumerate(pieces)], 1
            )
            return scores, lambda w: jnp.concatenate(
                [tn_dot(values(k), cut(w, i).astype(BF16)) for i, k in enumerate(pieces)], 1
            ), None
        owner = lax.broadcasted_iota(jnp.int32, (ct, steps * rest), 1) // rest
        scores = nt_dot(keys(0), queries)
        for s in range(1, steps):
            scores = jnp.where(owner == s, nt_dot(keys(s), queries), scores)

        def weigh(w):
            o = 0.0
            for s in range(steps):
                o = o + tn_dot(values(s), jnp.where(owner == s, w, 0.0).astype(BF16))
            return o

        return scores, weigh, None

    def own_state(h):
        for t, tile in enumerate(tiles):
            queries = query_tile(t, own_query(h))
            m, l, o = one_pass(part_of(scale, tile), [noisy(h, t, queries)])
            cols = slice(tile[0], tile[0] + tile[1])
            m_ref[h, :, cols], l_ref[h, :, cols], o_ref[h, :, cols] = m, l, o

    def own_update(j, h):
        visible = mask_ref[p, p - 1 - j]
        for t, tile in enumerate(tiles):
            queries = query_tile(t, own_query(h))
            cols = slice(tile[0], tile[0] + tile[1])
            old = m_ref[h, :, cols], l_ref[h, :, cols], o_ref[h, :, cols]
            block = plain(kv_ref[j, h, 0], kv_ref[j, h, 1], queries, visible)
            m, l, o = one_pass(part_of(scale, tile), [block], old)
            m_ref[h, :, cols], l_ref[h, :, cols], o_ref[h, :, cols] = m, l, o

    def finish_tile(h, t, averaged):
        lo, width, pieces = tiles[t]
        sq_ref[:, lo : lo + width] += jnp.sum(averaged * averaged, 0, keepdims=True)
        turned = jnp.transpose(averaged)
        at = 0
        for s, first, end in pieces:
            avg_ref[s, 0, first:end, head_cols(h)] = turned[at : at + end - first]
            at += end - first

    def finish_own(h):
        for t, tile in enumerate(tiles):
            cols = slice(tile[0], tile[0] + tile[1])
            finish_tile(h, t, o_ref[h, :, cols] * (1.0 / l_ref[h, :, cols]))

    fold = LANES // (steps * rest) if rest else 1

    def pack(h, t, o):
        lo, width, _ = tiles[t]
        if lo < split:
            for i in range(width // LANES):
                at = (lo // LANES + i) * HD
                osend_ref[h, at : at + HD, :] = o[:, i * LANES : (i + 1) * LANES].astype(BF16)
        else:
            high, at = HD // fold, split // LANES * HD
            pieces = [o[i * high : (i + 1) * high] for i in range(fold)]
            osend_ref[h, at : at + high, :] = jnp.concatenate(pieces, 1).astype(BF16)

    def unpack(h, t):
        lo, width, _ = tiles[t]
        if lo < split:
            pieces = []
            for i in range(width // LANES):
                at = (lo // LANES + i) * HD
                pieces.append(oin_ref[h, at : at + HD, :].astype(F32))
            return jnp.concatenate(pieces, 1)
        high, at = HD // fold, split // LANES * HD
        held = oin_ref[h, at : at + high, :].astype(F32)
        return jnp.concatenate([held[:, i * width : (i + 1) * width] for i in range(fold)], 0)

    def finish_last(h):
        ml_copy(h).wait_recv()
        o_copy(h).wait_recv()
        for t, tile in enumerate(tiles):
            cols = slice(tile[0], tile[0] + tile[1])
            mine, theirs = m_ref[h, :, cols], mlin_ref[h, 0, :, cols]
            m = jnp.maximum(mine, theirs)
            a, b = jnp.exp2(mine - m), jnp.exp2(theirs - m)
            inverse = 1.0 / (l_ref[h, :, cols] * a + mlin_ref[h, 1, :, cols] * b)
            finish_tile(h, t, o_ref[h, :, cols] * (a * inverse) + unpack(h, t) * (b * inverse))

    together = min(blocks, 3)

    def help_sums(h, c, first, queries, segment):
        def arrived(j):
            visible = mask_ref[segment, helper - 1 - j]
            return plain(kv_ref[j, h, 0], kv_ref[j, h, 1], queries, visible)

        sums = one_pass(c, [first] + [arrived(j) for j in range(together)])
        if blocks > together:
            sums = lax.fori_loop(
                together, blocks, lambda j, old: one_pass(c, [arrived(j)], old), sums
            )
        return sums

    def help_last(h):
        for t, tile in enumerate(tiles):
            queries = query_tile(t, last_query(h))
            own = plain(
                own_ref[0, 0, :, head_cols(h)], own_ref[1, 0, :, head_cols(h)], queries,
                mask_ref[last, helper],
            )
            m, l, o = help_sums(h, part_of(last_scale, tile), own, queries, last)
            cols = slice(tile[0], tile[0] + tile[1])
            mlsend_ref[h, 0, :, cols], mlsend_ref[h, 1, :, cols] = m, l
            pack(h, t, o)

    def help_own(h):
        for t, tile in enumerate(tiles):
            queries = query_tile(t, own_query(h))
            m, l, o = help_sums(h, part_of(scale, tile), noisy(h, t, queries), queries, helper)
            finish_tile(h, t, o * (1.0 / l))

    def gather_hidden():
        for d in range(1, group):
            part_copy(d).wait()
        summed = part_ref[g].astype(F32)
        for d in range(1, group):
            summed = summed + part_in[d - 1].astype(F32)
        hid_ref[...] = summed.astype(BF16)

        @pl.when(p < n - 1)
        def _():
            hid_copy.start()

    def update_all(h):
        lax.fori_loop(0, p, lambda j, c: (own_update(j, h), c)[1], 0)

    def first_heads(h):
        @pl.when(feeds & (h + ahead < heads))
        def _():
            pass_on(h + ahead)

        @pl.when(jnp.logical_not(helps) & (h == min(1, heads - 1)))
        def _():
            gather_hidden()

        @pl.when(helps)
        def _():
            @pl.when(h >= routed)
            def _():
                lax.fori_loop(0, blocks, lambda j, c: (arrive(j, h), c)[1], 0)
                lastq_copy(h).wait_recv()
                help_last(h)
                ml_copy(h).start()
                o_copy(h).start()

            help_own(h)

        @pl.when(jnp.logical_not(helps))
        def _():
            own_state(h)

        @pl.when(jnp.logical_not(helps | ends))
        def _():
            update_all(h)
            finish_own(h)

    def last_routed(h):
        lax.fori_loop(0, p, lambda j, c: (arrive(j, h), c)[1], 0)
        update_all(h)
        finish_own(h)

    def decode():
        loads[7].wait()

        @pl.when(p > 0)
        def _():
            hid_copy.wait_recv()

        @pl.when(p == 0)
        def _():
            prev_ref[...] = jnp.zeros_like(prev_ref)

        now = hid_ref[...].astype(F32)
        before = prev_ref[...].astype(F32)
        width = now.shape[1]
        frame = lax.rem(lax.broadcasted_iota(jnp.int32, (rp, width), 0), FR)
        mixed = jnp.zeros((2 * rp, width), F32)
        for k in range(KT):
            late = pltpu.roll(before, k, 0) if k else before
            if k:
                cur = jnp.where(
                    frame >= k, pltpu.roll(now, k, 0), pltpu.roll(before, rp + k - FR, 0)
                )
            else:
                cur = now
            window = jnp.concatenate([cur, late], 0).astype(BF16)
            mixed = mixed + jnp.dot(window, conv_ref[k], preferred_element_type=F32)
        frames = jax.nn.silu(mixed).astype(BF16).astype(F32)
        cur, late = frames[:rp], frames[rp:]
        fade = fade_ref[0]
        aligned = jnp.zeros_like(late)
        for count in range(1, FADE + 1):
            aligned = jnp.where(fade == count, pltpu.roll(late, rp - FR + count, 0), aligned)
        active = (frame < fade) & (p > 0)
        fade_f = fade.astype(F32)
        weight = (frame.astype(F32) + 1.0) / (jnp.zeros((rp, width), F32) + fade_f + 1.0)
        mix = weight * cur + (1.0 - weight) * aligned
        dec_ref[0] = jnp.where(active, mix, cur)[:rows].astype(BF16)

    sq_ref[...] = jnp.zeros_like(sq_ref)

    @pl.when(helps)
    def _():
        def hand_on_routed(j, carry):
            for h in range(routed):
                hand_on(j, h)
            return carry

        lax.fori_loop(0, min(blocks, 1), hand_on_routed, 0)
        gather_hidden()
        lax.fori_loop(min(blocks, 1), blocks, hand_on_routed, 0)

    every_head(first_heads)
    decode()

    @pl.when(ends)
    def _():
        for h in range(routed):
            last_routed(h)
        every_head(finish_last, routed)

    for d in range(1, group):
        stat_copy(d).start()
    for d in range(1, group):
        stat_copy(d).wait()
    squares = sq_ref[...]
    for d in range(1, group):
        squares = squares + stat_in[d - 1]
    inv_ref[...] = lax.rsqrt(squares / (HD * heads * group) + 1e-06)

    @pl.when(p < n - 1)
    def _():
        hid_copy.wait_send()

    def drain_kv(h):
        def one(j, carry):
            kv_copy(clean_hbm.at[:, 0, :, head_cols(h)], j, h).wait_send()
            return carry

        lax.fori_loop(0, p + 1, one, 0)

    @pl.when(feeds)
    def _():
        every_head(drain_kv)

    @pl.when(helps)
    def _():
        for h in range(routed):
            drain_kv(h)

        def drain(h):
            ml_copy(h).wait_send()
            o_copy(h).wait_send()

        every_head(drain, routed)

    @pl.when(ends)
    def _():
        every_head(lambda h: lastq_copy(h).wait_send(), routed)


def write_out(dims, avg_ref, inv_ref, dec_ref, att_hbm, dec_hbm, att_ref, sem):
    steps, ct, heads, main = dims
    rest, split = ct - main, steps * main
    dec_copy = pltpu.make_async_copy(dec_ref, dec_hbm, sem.at[steps])
    dec_copy.start()
    inverse = jnp.transpose(jnp.broadcast_to(inv_ref[...], (HD, steps * ct)))
    copies = []
    for s in range(steps):
        spans = [(0, main, s * main)] if main else []
        if rest:
            spans.append((main, ct, split + s * rest))
        for lo, hi, at in spans:
            for h in range(heads):
                cols = slice(h * HD, (h + 1) * HD)
                att_ref[s, 0, lo:hi, cols] = (
                    avg_ref[s, 0, lo:hi, cols] * inverse[at : at + hi - lo]
                ).astype(BF16)
        copy = pltpu.make_async_copy(att_ref.at[s], att_hbm.at[s], sem.at[s])
        copy.start()
        copies.append(copy)
    for copy in copies:
        copy.wait()
    dec_copy.wait()


def per_device(sizes, query, noisy_kv, clean_kv, causal_mask, step_index, finished, w_in, conv_w, fade_count):
    n, mp_n, seq_n = sizes
    group = mp_n * seq_n
    steps, _, ct, width = query.shape
    heads = width // HD
    channels = w_in.shape[1]
    rows = ct // group
    rp = -(-rows // 16) * 16
    main = ct // LANES * LANES
    total = steps * ct
    dims = (n, mp_n, seq_n, steps, ct, heads, rows, rp, main)
    vmem = pltpu.VMEM
    dma = pltpu.SemaphoreType.DMA
    hbm = pl.BlockSpec(memory_space=pltpu.HBM)
    out = pl.BlockSpec(memory_space=pltpu.VMEM)
    slots = max(n - 1, 1)
    arguments = [
        pltpu.with_memory_space_constraint(x, pltpu.HBM)
        for x in (causal_mask, step_index, query, noisy_kv, clean_kv, finished, w_in, conv_w)
    ]
    arguments.insert(2, fade_count)
    averaged, inverse, decoded = pl.pallas_call(
        functools.partial(kernel, dims),
        out_shape=(
            jax.ShapeDtypeStruct(query.shape, F32),
            jax.ShapeDtypeStruct((1, total), F32),
            jax.ShapeDtypeStruct((1, rows, channels), BF16),
        ),
        in_specs=[hbm] * 9,
        out_specs=(out, out, out),
        scratch_shapes=[
            vmem(query.shape, BF16),
            vmem(noisy_kv.shape, BF16),
            vmem(finished.shape, BF16),
            vmem(w_in.shape, BF16),
            vmem(conv_w.shape, BF16),
            vmem(clean_kv.shape, BF16),
            vmem((slots, heads, 2, ct, HD), BF16),
            vmem((heads, steps, ct, HD), BF16),
            vmem((heads, 1, total), F32),
            vmem((heads, 1, total), F32),
            vmem((heads, HD, total), F32),
            vmem((heads, total * HD // LANES, LANES), BF16),
            vmem((heads, total * HD // LANES, LANES), BF16),
            vmem((heads, 2, 1, total), F32),
            vmem((heads, 2, 1, total), F32),
            vmem((group, rp, channels), BF16),
            vmem((group - 1, rp, channels), BF16),
            vmem((rp, channels), BF16),
            vmem((rp, channels), BF16),
            vmem((1, total), F32),
            vmem((group - 1, 1, total), F32),
            pltpu.SMEM(causal_mask.shape, jnp.int32),
            pltpu.SMEM(step_index.shape, jnp.int32),
            pltpu.SMEM(fade_count.shape, jnp.int32),
            dma((9,)),
            dma((slots, heads)),
            dma((slots, heads)),
            dma((heads,)),
            dma((heads,)),
            dma((heads,)),
            dma((heads,)),
            dma((heads,)),
            dma((heads,)),
            dma((group - 1,)),
            dma((group - 1,)),
            dma,
            dma,
            dma((group - 1,)),
            dma((group - 1,)),
        ],
        compiler_params=pltpu.CompilerParams(
            collective_id=0, has_side_effects=True, vmem_limit_bytes=28 * 2**20
        ),
    )(*arguments)
    return pl.pallas_call(
        functools.partial(write_out, (steps, ct, heads, main)),
        out_shape=(
            jax.ShapeDtypeStruct(query.shape, BF16),
            jax.ShapeDtypeStruct(decoded.shape, BF16),
        ),
        in_specs=[out] * 3,
        out_specs=(hbm, hbm),
        scratch_shapes=[vmem(query.shape, BF16), dma((steps + 1,))],
        compiler_params=pltpu.CompilerParams(vmem_limit_bytes=8 * 2**20),
    )(averaged, inverse, decoded)


def solution(mesh):
    placed = (
        P(None, ("groups", "span"), None, ("mp", "seq")),
        P(None, None, ("groups", "span"), None, ("mp", "seq")),
        P(None, ("groups", "span"), None, ("mp", "seq")),
        P("groups", None),
        P("groups", None),
        P(("groups", "span"), None, ("mp", "seq")),
        P(("mp", "seq"), None),
        P(),
        P(("groups", "span")),
    )
    sizes = (mesh.shape["span"], mesh.shape["mp"], mesh.shape["seq"])
    return jax.shard_map(
        functools.partial(per_device, sizes),
        mesh=mesh,
        in_specs=placed,
        out_specs=(
            P(None, ("groups", "span"), None, ("mp", "seq")),
            P(("groups", "span"), ("mp", "seq"), None),
        ),
        check_vma=False,
    )
```

time: 39.3 us -> 35.4 us (0.901)
  Pallas kernels: 37.9 us -> 34 us
    pallas_call x1, Pallas kernels: 37 us -> 32.8 us  [per_device(): pl.pallas_call(functools.partial(kernel, dims), out_shape=(jax.ShapeDtype...]
where the time goes in v2:
time: 35.4 us; the launch traced here: 35.3 us
  Pallas kernels  34 us (96%)
  between operations  1.29 us (4%)
    pallas_call x1, Pallas kernels, per_device(): pl.pallas_call(functools.partial(kernel, dims), out_shape=(jax.ShapeDtype...  32.8 us
    pallas_call x1, Pallas kernels, per_device(): pl.pallas_call(functools.partial(write_out, (steps, ct, heads, main)), ou...  1.11 us

profile of v2, /device:TPU:29, one launch (start us, length us, event | category | flops | bytes accessed | tf_op | source)
XLA Modules:
  0.0 35.3 jit_solution(13690771536898491340)
XLA Ops:
  1.3 32.8 %shard_map.104 = (f32[4,1,144,768]{3,2,1,0:T(8,128)S(1)}, f32[1,576]{1,0:T(1,128)S(1)}, bf16[1,36,512]{2,1,0:T(8,128)(2,1)S(1)}) custom-call(s32[4,4]{1,0:T(4,128)} %mask_hbm.1, s32[4,4]{1,0:T(4,128)} %index_hbm.1, s32[1]{0:T(128)S(6)} %copy.11.fade_hbm, bf16[4,1,144,768]{3,2,1,0:T(8,128)(2,1)} %query_hbm.1, bf16[4,2,1,144,768]{4,3,2,1,0:T(8,128)(2,1)} %noisy_hbm.1, ...), custom_call_target="tpu_custom_call" | custom-call | tf_op jit(solution)/shard_map/pallas_call | solution.py:582
  34.1 1.1 %shard_map.105 = (bf16[4,1,144,768]{3,2,1,0:T(8,128)(2,1)}, bf16[1,36,512]{2,1,0:T(8,128)(2,1)}) custom-call(f32[4,1,144,768]{3,2,1,0:T(8,128)S(1)} %get-tuple-element.5.avg_ref, f32[1,576]{1,0:T(1,128)S(1)} %get-tuple-element.6.inv_ref, bf16[1,36,512]{2,1,0:T(8,128)(2,1)S(1)} %get-tuple-element.7.dec_ref), custom_call_target="tpu_custom_call" | custom-call | tf_op jit(solution)/shard_map/pallas_call | solution.py:636

commit v3 on v2

--- a/solution.py
+++ b/solution.py
@@ -39,9 +39,10 @@
     avg_ref, inv_ref, dec_ref,
     q_ref, noisy_ref, fin_ref, win_ref, conv_ref, own_ref, kv_ref, lastq_ref,
     m_ref, l_ref, o_ref, osend_ref, oin_ref, mlsend_ref, mlin_ref,
-    part_ref, part_in, hid_ref, prev_ref, sq_ref, stat_in, mask_ref, index_ref, fade_ref,
+    part_ref, part_in, hid_ref, prev_ref, sq_ref, stat_in, late_ref, late_in, late_sum, late_got, mask_ref, index_ref, fade_ref,
     load_sem, kv_send, kv_recv, lastq_send, lastq_recv, o_send, o_recv, ml_send, ml_recv,
     part_send, part_recv, hid_send, hid_recv, stat_send, stat_recv,
+    late_send, late_recv, back_send, back_recv, sum_send, sum_recv,
 ):
     n, mp_n, seq_n, steps, ct, heads, rows, rp, main = dims
     group = mp_n * seq_n
@@ -55,6 +56,7 @@
     ends = (p == last) & (n > 1)
     blocks = max(helper, 0)
     routed = min(2, heads) if n > 1 else 0
+    final = heads - 1 if n > 1 and heads > routed else heads
 
     def peer(d):
         other = lax.rem(g + d, group)
@@ -114,6 +116,28 @@
         return pltpu.make_async_remote_copy(
             src_ref=mlsend_ref.at[h], dst_ref=mlin_ref.at[h], send_sem=ml_send.at[h],
             recv_sem=ml_recv.at[h], device_id={"span": p + 1}, device_id_type=MESH,
+        )
+
+    def back_copies():
+        where = {"span": p - 1}
+        return [
+            pltpu.make_async_remote_copy(
+                src_ref=src.at[final], dst_ref=dst.at[final], send_sem=back_send.at[i],
+                recv_sem=back_recv.at[i], device_id=where, device_id_type=MESH,
+            )
+            for i, (src, dst) in enumerate(((mlsend_ref, mlin_ref), (osend_ref, oin_ref)))
+        ]
+
+    def late_copy(d):
+        return pltpu.make_async_remote_copy(
+            src_ref=late_ref, dst_ref=late_in.at[d - 1], send_sem=late_send.at[d - 1],
+            recv_sem=late_recv.at[d - 1], device_id=peer(d)[1], device_id_type=MESH,
+        )
+
+    def sum_copy():
+        return pltpu.make_async_remote_copy(
+            src_ref=late_sum, dst_ref=late_got, send_sem=sum_send, recv_sem=sum_recv,
+            device_id={"span": p + 1}, device_id_type=MESH,
         )
 
     def part_copy(d):
@@ -216,13 +240,9 @@
     scale = scale_row(p)
     last_scale = scale_row(last)
 
-    wide = 4
-    tiles = []
-    for s in range(0, steps if main else 0, wide):
-        held = range(s, min(s + wide, steps))
-        tiles.append((s * main, len(held) * main, [(k, 0, main) for k in held]))
-    if rest:
-        tiles.append((split, steps * rest, [(s, main, ct) for s in range(steps)]))
+    whole = [(s, 0, main) for s in range(steps if main else 0)]
+    tail = [(s, main, ct) for s in range(steps if rest else 0)]
+    tiles = [(0, total, whole + tail)]
 
     def query_tile(t, row):
         return jnp.concatenate([row(*piece) for piece in tiles[t][2]], 0)
@@ -244,12 +264,18 @@
         m = functools.reduce(jnp.maximum, tops)
         if old is not None:
             m = jnp.maximum(m, old[0])
-        l, o = 0.0, 0.0
-        for scores, values, visible in scored:
+        l, o, weights, values = 0.0, 0.0, [], []
+        for scores, held, visible in scored:
             base = m if visible is None else jnp.where(visible > 0, m, -LOW)
             w = jnp.exp2(scores * c - base)
             l = l + w.sum(0, keepdims=True)
-            o = o + values(w)
+            if callable(held):
+                o = o + held(w)
+            else:
+                weights.append(w.astype(BF16))
+                values.append(held)
+        if values:
+            o = o + tn_dot(jnp.concatenate(values, 0), jnp.concatenate(weights, 0))
         if old is not None:
             factor = jnp.exp2(old[0] - m)
             l = l + old[1] * factor
@@ -257,32 +283,32 @@
         return m, l, o
 
     def plain(keys, values, queries, visible):
-        return nt_dot(keys, queries), lambda w: tn_dot(values, w.astype(BF16)), visible
+        return nt_dot(keys, queries), values, visible
 
     def noisy(h, t, queries):
         keys = lambda s: noisy_ref[s, 0, 0, :, head_cols(h)]
         values = lambda s: noisy_ref[s, 1, 0, :, head_cols(h)]
-        if tiles[t][0] < split:
-            pieces = [k for k, _, _ in tiles[t][2]]
-            cut = lambda x, i: x[:, i * main : (i + 1) * main]
-            scores = jnp.concatenate(
-                [nt_dot(keys(k), queries[i * main : (i + 1) * main]) for i, k in enumerate(pieces)], 1
-            )
-            return scores, lambda w: jnp.concatenate(
-                [tn_dot(values(k), cut(w, i).astype(BF16)) for i, k in enumerate(pieces)], 1
-            ), None
-        owner = lax.broadcasted_iota(jnp.int32, (ct, steps * rest), 1) // rest
-        scores = nt_dot(keys(0), queries)
-        for s in range(1, steps):
-            scores = jnp.where(owner == s, nt_dot(keys(s), queries), scores)
+        cut = lambda k: slice(k * main, (k + 1) * main)
+        scores = [nt_dot(keys(k), queries[cut(k)]) for k, _, _ in whole]
+        if tail:
+            owner = lax.broadcasted_iota(jnp.int32, (ct, steps * rest), 1) // rest
+            every = nt_dot(jnp.concatenate([keys(s) for s in range(steps)], 0), queries[split:])
+            picked = every[0:ct]
+            for s in range(1, steps):
+                picked = jnp.where(owner == s, every[s * ct : (s + 1) * ct], picked)
+            scores.append(picked)
 
         def weigh(w):
-            o = 0.0
-            for s in range(steps):
-                o = o + tn_dot(values(s), jnp.where(owner == s, w, 0.0).astype(BF16))
-            return o
-
-        return scores, weigh, None
+            o = [tn_dot(values(k), w[:, cut(k)].astype(BF16)) for k, _, _ in whole]
+            if tail:
+                late = w[:, split:]
+                mine = [jnp.where(owner == s, late, 0.0).astype(BF16) for s in range(steps)]
+                o.append(
+                    tn_dot(jnp.concatenate([values(s) for s in range(steps)], 0), jnp.concatenate(mine, 0))
+                )
+            return jnp.concatenate(o, 1)
+
+        return jnp.concatenate(scores, 1), weigh, None
 
     def own_state(h):
         for t, tile in enumerate(tiles):
@@ -301,9 +327,10 @@
             m, l, o = one_pass(part_of(scale, tile), [block], old)
             m_ref[h, :, cols], l_ref[h, :, cols], o_ref[h, :, cols] = m, l, o
 
-    def finish_tile(h, t, averaged):
+    def finish_tile(h, t, averaged, count=True):
         lo, width, pieces = tiles[t]
-        sq_ref[:, lo : lo + width] += jnp.sum(averaged * averaged, 0, keepdims=True)
+        if count:
+            sq_ref[:, lo : lo + width] += jnp.sum(averaged * averaged, 0, keepdims=True)
         turned = jnp.transpose(averaged)
         at = 0
         for s, first, end in pieces:
@@ -318,27 +345,24 @@
     fold = LANES // (steps * rest) if rest else 1
 
     def pack(h, t, o):
-        lo, width, _ = tiles[t]
-        if lo < split:
-            for i in range(width // LANES):
-                at = (lo // LANES + i) * HD
-                osend_ref[h, at : at + HD, :] = o[:, i * LANES : (i + 1) * LANES].astype(BF16)
-        else:
+        for i in range(split // LANES):
+            osend_ref[h, i * HD : (i + 1) * HD, :] = o[:, i * LANES : (i + 1) * LANES].astype(BF16)
+        if rest:
             high, at = HD // fold, split // LANES * HD
-            pieces = [o[i * high : (i + 1) * high] for i in range(fold)]
+            pieces = [o[i * high : (i + 1) * high, split:] for i in range(fold)]
             osend_ref[h, at : at + high, :] = jnp.concatenate(pieces, 1).astype(BF16)
 
     def unpack(h, t):
-        lo, width, _ = tiles[t]
-        if lo < split:
-            pieces = []
-            for i in range(width // LANES):
-                at = (lo // LANES + i) * HD
-                pieces.append(oin_ref[h, at : at + HD, :].astype(F32))
-            return jnp.concatenate(pieces, 1)
-        high, at = HD // fold, split // LANES * HD
-        held = oin_ref[h, at : at + high, :].astype(F32)
-        return jnp.concatenate([held[:, i * width : (i + 1) * width] for i in range(fold)], 0)
+        pieces = [
+            oin_ref[h, i * HD : (i + 1) * HD, :].astype(F32) for i in range(split // LANES)
+        ]
+        if rest:
+            high, at, width = HD // fold, split // LANES * HD, steps * rest
+            held = oin_ref[h, at : at + high, :].astype(F32)
+            pieces.append(
+                jnp.concatenate([held[:, i * width : (i + 1) * width] for i in range(fold)], 0)
+            )
+        return jnp.concatenate(pieces, 1)
 
     def finish_last(h):
         ml_copy(h).wait_recv()
@@ -353,28 +377,35 @@
 
     together = min(blocks, 3)
 
-    def help_sums(h, c, first, queries, segment):
+    def help_sums(h, c, first, queries, segment, old=None):
         def arrived(j):
             visible = mask_ref[segment, helper - 1 - j]
             return plain(kv_ref[j, h, 0], kv_ref[j, h, 1], queries, visible)
 
-        sums = one_pass(c, [first] + [arrived(j) for j in range(together)])
+        sums = one_pass(c, [first] + [arrived(j) for j in range(together)], old)
         if blocks > together:
             sums = lax.fori_loop(
                 together, blocks, lambda j, old: one_pass(c, [arrived(j)], old), sums
             )
         return sums
 
-    def help_last(h):
+    def help_last(h, closing=False):
         for t, tile in enumerate(tiles):
             queries = query_tile(t, last_query(h))
+            cols = slice(tile[0], tile[0] + tile[1])
+            old = None
+            if closing:
+                old = mlin_ref[h, 0, :, cols], mlin_ref[h, 1, :, cols], unpack(h, t)
             own = plain(
                 own_ref[0, 0, :, head_cols(h)], own_ref[1, 0, :, head_cols(h)], queries,
                 mask_ref[last, helper],
             )
-            m, l, o = help_sums(h, part_of(last_scale, tile), own, queries, last)
-            cols = slice(tile[0], tile[0] + tile[1])
-            mlsend_ref[h, 0, :, cols], mlsend_ref[h, 1, :, cols] = m, l
+            m, l, o = help_sums(h, part_of(last_scale, tile), own, queries, last, old)
+            if closing:
+                o = o * (1.0 / l)
+                late_ref[:, cols] = jnp.sum(o * o, 0, keepdims=True)
+            else:
+                mlsend_ref[h, 0, :, cols], mlsend_ref[h, 1, :, cols] = m, l
             pack(h, t, o)
 
     def help_own(h):
@@ -391,10 +422,6 @@
             summed = summed + part_in[d - 1].astype(F32)
         hid_ref[...] = summed.astype(BF16)
 
-        @pl.when(p < n - 1)
-        def _():
-            hid_copy.start()
-
     def update_all(h):
         lax.fori_loop(0, p, lambda j, c: (own_update(j, h), c)[1], 0)
 
@@ -413,9 +440,23 @@
             def _():
                 lax.fori_loop(0, blocks, lambda j, c: (arrive(j, h), c)[1], 0)
                 lastq_copy(h).wait_recv()
+
+            @pl.when((h >= routed) & (h < final))
+            def _():
                 help_last(h)
                 ml_copy(h).start()
                 o_copy(h).start()
+
+            if final < heads:
+
+                @pl.when(h == final)
+                def _():
+                    for copy in back_copies():
+                        copy.wait_recv()
+                    help_last(final, True)
+                    o_copy(final).start()
+                    for d in range(1, group):
+                        late_copy(d).start()
 
             help_own(h)
 
@@ -482,25 +523,73 @@
 
         lax.fori_loop(0, min(blocks, 1), hand_on_routed, 0)
         gather_hidden()
+        hid_copy.start()
         lax.fori_loop(min(blocks, 1), blocks, hand_on_routed, 0)
 
     every_head(first_heads)
-    decode()
+
+    @pl.when(feeds)
+    def _():
+        hid_copy.start()
+
+    @pl.when(ends)
+    def _():
+        if final < heads:
+            for t, tile in enumerate(tiles):
+                cols = slice(tile[0], tile[0] + tile[1])
+                pack(final, t, o_ref[final, :, cols])
+            mlsend_ref[final, 0] = m_ref[final]
+            mlsend_ref[final, 1] = l_ref[final]
+            for copy in back_copies():
+                copy.start()
+
+    @pl.when(jnp.logical_not(helps))
+    def _():
+        decode()
 
     @pl.when(ends)
     def _():
         for h in range(routed):
             last_routed(h)
-        every_head(finish_last, routed)
+        lax.fori_loop(routed, final, lambda h, c: (finish_last(h), c)[1], 0)
 
     for d in range(1, group):
         stat_copy(d).start()
+
+    @pl.when(helps)
+    def _():
+        decode()
+        if final < heads:
+            sums = late_ref[...]
+            for d in range(1, group):
+                late_copy(d).wait_recv()
+                sums = sums + late_in[d - 1]
+            late_sum[...] = sums
+            sum_copy().start()
+
     for d in range(1, group):
         stat_copy(d).wait()
     squares = sq_ref[...]
     for d in range(1, group):
         squares = squares + stat_in[d - 1]
-    inv_ref[...] = lax.rsqrt(squares / (HD * heads * group) + 1e-06)
+
+    def invert(sums):
+        inv_ref[...] = lax.rsqrt(sums / (HD * heads * group) + 1e-06)
+
+    @pl.when(jnp.logical_not(ends))
+    def _():
+        invert(squares)
+
+    @pl.when(ends)
+    def _():
+        if final < heads:
+            o_copy(final).wait_recv()
+            for t in range(len(tiles)):
+                finish_tile(final, t, unpack(final, t), False)
+            sum_copy().wait_recv()
+            invert(squares + late_got[...])
+        else:
+            invert(squares)
 
     @pl.when(p < n - 1)
     def _():
@@ -526,11 +615,19 @@
             ml_copy(h).wait_send()
             o_copy(h).wait_send()
 
-        every_head(drain, routed)
+        lax.fori_loop(routed, final, lambda h, c: (drain(h), c)[1], 0)
+        if final < heads:
+            o_copy(final).wait_send()
+            for d in range(1, group):
+                late_copy(d).wait_send()
+            sum_copy().wait_send()
 
     @pl.when(ends)
     def _():
         every_head(lambda h: lastq_copy(h).wait_send(), routed)
+        if final < heads:
+            for copy in back_copies():
+                copy.wait_send()
 
 
 def write_out(dims, avg_ref, inv_ref, dec_ref, att_hbm, dec_hbm, att_ref, sem):
@@ -610,6 +707,10 @@
             vmem((rp, channels), BF16),
             vmem((1, total), F32),
             vmem((group - 1, 1, total), F32),
+            vmem((1, total), F32),
+            vmem((group - 1, 1, total), F32),
+            vmem((1, total), F32),
+            vmem((1, total), F32),
             pltpu.SMEM(causal_mask.shape, jnp.int32),
             pltpu.SMEM(step_index.shape, jnp.int32),
             pltpu.SMEM(fade_count.shape, jnp.int32),
@@ -628,6 +729,12 @@
             dma,
             dma((group - 1,)),
             dma((group - 1,)),
+            dma((group - 1,)),
+            dma((group - 1,)),
+            dma((2,)),
+            dma((2,)),
+            dma,
+            dma,
         ],
         compiler_params=pltpu.CompilerParams(
             collective_id=0, has_side_effects=True, vmem_limit_bytes=28 * 2**20

time: 35.4 us -> 32.9 us (0.929)
  Pallas kernels: 34 us -> 31.4 us
    pallas_call x1, Pallas kernels: 32.8 us -> 30.3 us  [per_device(): pl.pallas_call(functools.partial(kernel, dims), out_shape=(jax.ShapeDtype...]
where the time goes in v3:
time: 32.9 us; the launch traced here: 32.7 us
  Pallas kernels  31.4 us (95%)
  between operations  1.29 us (4%)
    pallas_call x1, Pallas kernels, per_device(): pl.pallas_call(functools.partial(kernel, dims), out_shape=(jax.ShapeDtype...  30.3 us
    pallas_call x1, Pallas kernels, per_device(): pl.pallas_call(functools.partial(write_out, (steps, ct, heads, main)), ou...  1.11 us

profile of v3, /device:TPU:29, one launch (start us, length us, event | category | flops | bytes accessed | tf_op | source)
XLA Modules:
  0.0 32.7 jit_solution(5603643604863018422)
XLA Ops:
  1.3 30.3 %shard_map.104 = (f32[4,1,144,768]{3,2,1,0:T(8,128)S(1)}, f32[1,576]{1,0:T(1,128)S(1)}, bf16[1,36,512]{2,1,0:T(8,128)(2,1)S(1)}) custom-call(s32[4,4]{1,0:T(4,128)} %mask_hbm.1, s32[4,4]{1,0:T(4,128)} %index_hbm.1, s32[1]{0:T(128)S(6)} %copy.11.fade_hbm, bf16[4,1,144,768]{3,2,1,0:T(8,128)(2,1)} %query_hbm.1, bf16[4,2,1,144,768]{4,3,2,1,0:T(8,128)(2,1)} %noisy_hbm.1, ...), custom_call_target="tpu_custom_call" | custom-call | tf_op jit(solution)/shard_map/pallas_call | solution.py:679
  31.6 1.1 %shard_map.105 = (bf16[4,1,144,768]{3,2,1,0:T(8,128)(2,1)}, bf16[1,36,512]{2,1,0:T(8,128)(2,1)}) custom-call(f32[4,1,144,768]{3,2,1,0:T(8,128)S(1)} %get-tuple-element.5.avg_ref, f32[1,576]{1,0:T(1,128)S(1)} %get-tuple-element.6.inv_ref, bf16[1,36,512]{2,1,0:T(8,128)(2,1)S(1)} %get-tuple-element.7.dec_ref), custom_call_target="tpu_custom_call" | custom-call | tf_op jit(solution)/shard_map/pallas_call | solution.py:743

commit v4 on v3

--- a/solution.py
+++ b/solution.py
@@ -375,21 +375,24 @@
             inverse = 1.0 / (l_ref[h, :, cols] * a + mlin_ref[h, 1, :, cols] * b)
             finish_tile(h, t, o_ref[h, :, cols] * (a * inverse) + unpack(h, t) * (b * inverse))
 
-    together = min(blocks, 3)
-
-    def help_sums(h, c, first, queries, segment, old=None):
-        def arrived(j):
-            visible = mask_ref[segment, helper - 1 - j]
-            return plain(kv_ref[j, h, 0], kv_ref[j, h, 1], queries, visible)
-
-        sums = one_pass(c, [first] + [arrived(j) for j in range(together)], old)
-        if blocks > together:
+    def arrived(h, j, queries, segment):
+        visible = mask_ref[segment, helper - 1 - j]
+        return plain(kv_ref[j, h, 0], kv_ref[j, h, 1], queries, visible)
+
+    def help_sums(h, c, first, queries, segment, count, old=None):
+        together = min(count, 3)
+        held = [first] + [arrived(h, j, queries, segment) for j in range(together)]
+        sums = one_pass(c, held, old)
+        if count > together:
             sums = lax.fori_loop(
-                together, blocks, lambda j, old: one_pass(c, [arrived(j)], old), sums
+                together, count,
+                lambda j, so_far: one_pass(c, [arrived(h, j, queries, segment)], so_far), sums,
             )
         return sums
 
     def help_last(h, closing=False):
+        early = max(blocks - 1, 0)
+        lax.fori_loop(0, early, lambda j, c: (arrive(j, h), c)[1], 0)
         for t, tile in enumerate(tiles):
             queries = query_tile(t, last_query(h))
             cols = slice(tile[0], tile[0] + tile[1])
@@ -400,7 +403,17 @@
                 own_ref[0, 0, :, head_cols(h)], own_ref[1, 0, :, head_cols(h)], queries,
                 mask_ref[last, helper],
             )
-            m, l, o = help_sums(h, part_of(last_scale, tile), own, queries, last, old)
+            m, l, o = help_sums(h, part_of(last_scale, tile), own, queries, last, early, old)
+            m_ref[h, :, cols], l_ref[h, :, cols], o_ref[h, :, cols] = m, l, o
+        if blocks:
+            arrive(blocks - 1, h)
+        for t, tile in enumerate(tiles):
+            queries = query_tile(t, last_query(h))
+            cols = slice(tile[0], tile[0] + tile[1])
+            m, l, o = m_ref[h, :, cols], l_ref[h, :, cols], o_ref[h, :, cols]
+            if blocks:
+                block = arrived(h, blocks - 1, queries, last)
+                m, l, o = one_pass(part_of(last_scale, tile), [block], (m, l, o))
             if closing:
                 o = o * (1.0 / l)
                 late_ref[:, cols] = jnp.sum(o * o, 0, keepdims=True)
@@ -411,7 +424,8 @@
     def help_own(h):
         for t, tile in enumerate(tiles):
             queries = query_tile(t, own_query(h))
-            m, l, o = help_sums(h, part_of(scale, tile), noisy(h, t, queries), queries, helper)
+            first = noisy(h, t, queries)
+            m, l, o = help_sums(h, part_of(scale, tile), first, queries, helper, blocks)
             finish_tile(h, t, o * (1.0 / l))
 
     def gather_hidden():
@@ -438,7 +452,6 @@
         def _():
             @pl.when(h >= routed)
             def _():
-                lax.fori_loop(0, blocks, lambda j, c: (arrive(j, h), c)[1], 0)
                 lastq_copy(h).wait_recv()
 
             @pl.when((h >= routed) & (h < final))
@@ -567,8 +580,16 @@
             late_sum[...] = sums
             sum_copy().start()
 
+    if final < heads:
+
+        @pl.when(ends)
+        def _():
+            o_copy(final).wait_recv()
+            for t in range(len(tiles)):
+                finish_tile(final, t, unpack(final, t), False)
+
     for d in range(1, group):
-        stat_copy(d).wait()
+        stat_copy(d).wait_recv()
     squares = sq_ref[...]
     for d in range(1, group):
         squares = squares + stat_in[d - 1]
@@ -583,13 +604,13 @@
     @pl.when(ends)
     def _():
         if final < heads:
-            o_copy(final).wait_recv()
-            for t in range(len(tiles)):
-                finish_tile(final, t, unpack(final, t), False)
             sum_copy().wait_recv()
             invert(squares + late_got[...])
         else:
             invert(squares)
+
+    for d in range(1, group):
+        stat_copy(d).wait_send()
 
     @pl.when(p < n - 1)
     def _():
@@ -635,9 +656,11 @@
     rest, split = ct - main, steps * main
     dec_copy = pltpu.make_async_copy(dec_ref, dec_hbm, sem.at[steps])
     dec_copy.start()
-    inverse = jnp.transpose(jnp.broadcast_to(inv_ref[...], (HD, steps * ct)))
+    turned = lambda lo, hi: jnp.transpose(jnp.broadcast_to(inv_ref[:, lo:hi], (HD, hi - lo)))
+    late = turned(split, steps * ct) if rest else None
     copies = []
     for s in range(steps):
+        inverse = turned(s * main, (s + 1) * main) if main else None
         spans = [(0, main, s * main)] if main else []
         if rest:
             spans.append((main, ct, split + s * rest))
@@ -645,7 +668,7 @@
             for h in range(heads):
                 cols = slice(h * HD, (h + 1) * HD)
                 att_ref[s, 0, lo:hi, cols] = (
-                    avg_ref[s, 0, lo:hi, cols] * inverse[at : at + hi - lo]
+                    avg_ref[s, 0, lo:hi, cols] * (late[at - split : at - split + hi - lo] if lo else inverse)
                 ).astype(BF16)
         copy = pltpu.make_async_copy(att_ref.at[s], att_hbm.at[s], sem.at[s])
         copy.start()

time: 32.9 us -> 32.4 us (0.985)
  Pallas kernels: 31.4 us -> 30.9 us
    pallas_call x1, Pallas kernels: 30.3 us -> 29.9 us  [per_device(): pl.pallas_call(functools.partial(kernel, dims), out_shape=(jax.ShapeDtype...]
where the time goes in v4:
time: 32.4 us; the launch traced here: 32.2 us
  Pallas kernels  30.9 us (95%)
  between operations  1.29 us (4%)
    pallas_call x1, Pallas kernels, per_device(): pl.pallas_call(functools.partial(kernel, dims), out_shape=(jax.ShapeDtype...  29.9 us
    pallas_call x1, Pallas kernels, per_device(): pl.pallas_call(functools.partial(write_out, (steps, ct, heads, main)), ou...  1.06 us

profile of v4, /device:TPU:29, one launch (start us, length us, event | category | flops | bytes accessed | tf_op | source)
XLA Modules:
  0.0 32.2 jit_solution(10099108595378126723)
XLA Ops:
  1.3 29.9 %shard_map.104 = (f32[4,1,144,768]{3,2,1,0:T(8,128)S(1)}, f32[1,576]{1,0:T(1,128)S(1)}, bf16[1,36,512]{2,1,0:T(8,128)(2,1)S(1)}) custom-call(s32[4,4]{1,0:T(4,128)} %mask_hbm.1, s32[4,4]{1,0:T(4,128)} %index_hbm.1, s32[1]{0:T(128)S(6)} %copy.11.fade_hbm, bf16[4,1,144,768]{3,2,1,0:T(8,128)(2,1)} %query_hbm.1, bf16[4,2,1,144,768]{4,3,2,1,0:T(8,128)(2,1)} %noisy_hbm.1, ...), custom_call_target="tpu_custom_call" | custom-call | tf_op jit(solution)/shard_map/pallas_call | solution.py:702
  31.2 1.1 %shard_map.105 = (bf16[4,1,144,768]{3,2,1,0:T(8,128)(2,1)}, bf16[1,36,512]{2,1,0:T(8,128)(2,1)}) custom-call(f32[4,1,144,768]{3,2,1,0:T(8,128)S(1)} %get-tuple-element.5.avg_ref, f32[1,576]{1,0:T(1,128)S(1)} %get-tuple-element.6.inv_ref, bf16[1,36,512]{2,1,0:T(8,128)(2,1)S(1)} %get-tuple-element.7.dec_ref), custom_call_target="tpu_custom_call" | custom-call | tf_op jit(solution)/shard_map/pallas_call | solution.py:766

commit v5 on v4

--- a/solution.py
+++ b/solution.py
@@ -56,7 +56,7 @@
     ends = (p == last) & (n > 1)
     blocks = max(helper, 0)
     routed = min(2, heads) if n > 1 else 0
-    final = heads - 1 if n > 1 and heads > routed else heads
+    final = max(routed, heads - 2) if n > 1 else heads
 
     def peer(d):
         other = lax.rem(g + d, group)
@@ -118,12 +118,12 @@
             recv_sem=ml_recv.at[h], device_id={"span": p + 1}, device_id_type=MESH,
         )
 
-    def back_copies():
+    def back_copies(h):
         where = {"span": p - 1}
         return [
             pltpu.make_async_remote_copy(
-                src_ref=src.at[final], dst_ref=dst.at[final], send_sem=back_send.at[i],
-                recv_sem=back_recv.at[i], device_id=where, device_id_type=MESH,
+                src_ref=src.at[h], dst_ref=dst.at[h], send_sem=back_send.at[i, h],
+                recv_sem=back_recv.at[i, h], device_id=where, device_id_type=MESH,
             )
             for i, (src, dst) in enumerate(((mlsend_ref, mlin_ref), (osend_ref, oin_ref)))
         ]
@@ -379,10 +379,10 @@
         visible = mask_ref[segment, helper - 1 - j]
         return plain(kv_ref[j, h, 0], kv_ref[j, h, 1], queries, visible)
 
-    def help_sums(h, c, first, queries, segment, count, old=None):
+    def help_sums(h, c, first, queries, segment, count):
         together = min(count, 3)
         held = [first] + [arrived(h, j, queries, segment) for j in range(together)]
-        sums = one_pass(c, held, old)
+        sums = one_pass(c, held)
         if count > together:
             sums = lax.fori_loop(
                 together, count,
@@ -396,17 +396,17 @@
         for t, tile in enumerate(tiles):
             queries = query_tile(t, last_query(h))
             cols = slice(tile[0], tile[0] + tile[1])
-            old = None
-            if closing:
-                old = mlin_ref[h, 0, :, cols], mlin_ref[h, 1, :, cols], unpack(h, t)
             own = plain(
                 own_ref[0, 0, :, head_cols(h)], own_ref[1, 0, :, head_cols(h)], queries,
                 mask_ref[last, helper],
             )
-            m, l, o = help_sums(h, part_of(last_scale, tile), own, queries, last, early, old)
+            m, l, o = help_sums(h, part_of(last_scale, tile), own, queries, last, early)
             m_ref[h, :, cols], l_ref[h, :, cols], o_ref[h, :, cols] = m, l, o
         if blocks:
             arrive(blocks - 1, h)
+        if closing:
+            for copy in back_copies(h):
+                copy.wait_recv()
         for t, tile in enumerate(tiles):
             queries = query_tile(t, last_query(h))
             cols = slice(tile[0], tile[0] + tile[1])
@@ -415,8 +415,12 @@
                 block = arrived(h, blocks - 1, queries, last)
                 m, l, o = one_pass(part_of(last_scale, tile), [block], (m, l, o))
             if closing:
-                o = o * (1.0 / l)
-                late_ref[:, cols] = jnp.sum(o * o, 0, keepdims=True)
+                mine = mlin_ref[h, 0, :, cols]
+                top = jnp.maximum(m, mine)
+                a, b = jnp.exp2(m - top), jnp.exp2(mine - top)
+                inverse = 1.0 / (l * a + mlin_ref[h, 1, :, cols] * b)
+                o = o * (a * inverse) + unpack(h, t) * (b * inverse)
+                late_ref[:, cols] += jnp.sum(o * o, 0, keepdims=True)
             else:
                 mlsend_ref[h, 0, :, cols], mlsend_ref[h, 1, :, cols] = m, l
             pack(h, t, o)
@@ -462,12 +466,13 @@
 
             if final < heads:
 
-                @pl.when(h == final)
+                @pl.when(h >= final)
                 def _():
-                    for copy in back_copies():
-                        copy.wait_recv()
-                    help_last(final, True)
-                    o_copy(final).start()
+                    help_last(h, True)
+                    o_copy(h).start()
+
+                @pl.when(h == heads - 1)
+                def _():
                     for d in range(1, group):
                         late_copy(d).start()
 
@@ -526,6 +531,7 @@
         dec_ref[0] = jnp.where(active, mix, cur)[:rows].astype(BF16)
 
     sq_ref[...] = jnp.zeros_like(sq_ref)
+    late_ref[...] = jnp.zeros_like(late_ref)
 
     @pl.when(helps)
     def _():
@@ -547,14 +553,16 @@
 
     @pl.when(ends)
     def _():
-        if final < heads:
+        def send_back(h):
             for t, tile in enumerate(tiles):
                 cols = slice(tile[0], tile[0] + tile[1])
-                pack(final, t, o_ref[final, :, cols])
-            mlsend_ref[final, 0] = m_ref[final]
-            mlsend_ref[final, 1] = l_ref[final]
-            for copy in back_copies():
+                pack(h, t, o_ref[h, :, cols])
+            mlsend_ref[h, 0] = m_ref[h]
+            mlsend_ref[h, 1] = l_ref[h]
+            for copy in back_copies(h):
                 copy.start()
+
+        every_head(send_back, final)
 
     @pl.when(jnp.logical_not(helps))
     def _():
@@ -584,9 +592,12 @@
 
         @pl.when(ends)
         def _():
-            o_copy(final).wait_recv()
-            for t in range(len(tiles)):
-                finish_tile(final, t, unpack(final, t), False)
+            def finish_late(h):
+                o_copy(h).wait_recv()
+                for t in range(len(tiles)):
+                    finish_tile(h, t, unpack(h, t), False)
+
+            every_head(finish_late, final)
 
     for d in range(1, group):
         stat_copy(d).wait_recv()
@@ -638,7 +649,7 @@
 
         lax.fori_loop(routed, final, lambda h, c: (drain(h), c)[1], 0)
         if final < heads:
-            o_copy(final).wait_send()
+            every_head(lambda h: o_copy(h).wait_send(), final)
             for d in range(1, group):
                 late_copy(d).wait_send()
             sum_copy().wait_send()
@@ -646,9 +657,12 @@
     @pl.when(ends)
     def _():
         every_head(lambda h: lastq_copy(h).wait_send(), routed)
-        if final < heads:
-            for copy in back_copies():
+
+        def drain_back(h):
+            for copy in back_copies(h):
                 copy.wait_send()
+
+        every_head(drain_back, final)
 
 
 def write_out(dims, avg_ref, inv_ref, dec_ref, att_hbm, dec_hbm, att_ref, sem):
@@ -754,8 +768,8 @@
             dma((group - 1,)),
             dma((group - 1,)),
             dma((group - 1,)),
-            dma((2,)),
-            dma((2,)),
+            dma((2, heads)),
+            dma((2, heads)),
             dma,
             dma,
         ],

time: 32.4 us -> 32 us (0.988); the launches traced: 32.2 us -> 31.5 us
  Pallas kernels: 30.9 us -> 30.2 us
    pallas_call x1, Pallas kernels: 29.9 us -> 29.1 us  [per_device(): pl.pallas_call(functools.partial(kernel, dims), out_shape=(jax.ShapeDtype...]
where the time goes in v5:
time: 32 us; the launch traced here: 31.5 us
  Pallas kernels  30.2 us (94%)
  between operations  1.29 us (4%)
    pallas_call x1, Pallas kernels, per_device(): pl.pallas_call(functools.partial(kernel, dims), out_shape=(jax.ShapeDtype...  29.1 us
    pallas_call x1, Pallas kernels, per_device(): pl.pallas_call(functools.partial(write_out, (steps, ct, heads, main)), ou...  1.06 us

profile of v5, /device:TPU:29, one launch (start us, length us, event | category | flops | bytes accessed | tf_op | source)
XLA Modules:
  0.0 31.5 jit_solution(5880883843456632586)
XLA Ops:
  1.3 29.1 %shard_map.104 = (f32[4,1,144,768]{3,2,1,0:T(8,128)S(1)}, f32[1,576]{1,0:T(1,128)S(1)}, bf16[1,36,512]{2,1,0:T(8,128)(2,1)S(1)}) custom-call(s32[4,4]{1,0:T(4,128)} %mask_hbm.1, s32[4,4]{1,0:T(4,128)} %index_hbm.1, s32[1]{0:T(128)S(6)} %copy.11.fade_hbm, bf16[4,1,144,768]{3,2,1,0:T(8,128)(2,1)} %query_hbm.1, bf16[4,2,1,144,768]{4,3,2,1,0:T(8,128)(2,1)} %noisy_hbm.1, ...), custom_call_target="tpu_custom_call" | custom-call | tf_op jit(solution)/shard_map/pallas_call | solution.py:716
  30.4 1.1 %shard_map.105 = (bf16[4,1,144,768]{3,2,1,0:T(8,128)(2,1)}, bf16[1,36,512]{2,1,0:T(8,128)(2,1)}) custom-call(f32[4,1,144,768]{3,2,1,0:T(8,128)S(1)} %get-tuple-element.5.avg_ref, f32[1,576]{1,0:T(1,128)S(1)} %get-tuple-element.6.inv_ref, bf16[1,36,512]{2,1,0:T(8,128)(2,1)S(1)} %get-tuple-element.7.dec_ref), custom_call_target="tpu_custom_call" | custom-call | tf_op jit(solution)/shard_map/pallas_call | solution.py:780

commit v6 on v5

--- a/solution.py
+++ b/solution.py
@@ -588,6 +588,16 @@
             late_sum[...] = sums
             sum_copy().start()
 
+    @pl.when(ends)
+    def _():
+        every_head(lambda h: lastq_copy(h).wait_send(), routed)
+
+        def drain_back(h):
+            for copy in back_copies(h):
+                copy.wait_send()
+
+        every_head(drain_back, final)
+
     if final < heads:
 
         @pl.when(ends)
@@ -653,16 +663,6 @@
             for d in range(1, group):
                 late_copy(d).wait_send()
             sum_copy().wait_send()
-
-    @pl.when(ends)
-    def _():
-        every_head(lambda h: lastq_copy(h).wait_send(), routed)
-
-        def drain_back(h):
-            for copy in back_copies(h):
-                copy.wait_send()
-
-        every_head(drain_back, final)
 
 
 def write_out(dims, avg_ref, inv_ref, dec_ref, att_hbm, dec_hbm, att_ref, sem):

time: 32 us -> 32 us (level)
  no operation moved by 1% of the time
where the time goes in v6:
time: 32 us; the launch traced here: 31.5 us
  Pallas kernels  30.2 us (94%)
  between operations  1.29 us (4%)
    pallas_call x1, Pallas kernels, per_device(): pl.pallas_call(functools.partial(kernel, dims), out_shape=(jax.ShapeDtype...  29.1 us
    pallas_call x1, Pallas kernels, per_device(): pl.pallas_call(functools.partial(write_out, (steps, ct, heads, main)), ou...  1.06 us

profile of v6, /device:TPU:29, one launch (start us, length us, event | category | flops | bytes accessed | tf_op | source)
XLA Modules:
  0.0 31.5 jit_solution(12991785418805281183)
XLA Ops:
  1.3 29.1 %shard_map.104 = (f32[4,1,144,768]{3,2,1,0:T(8,128)S(1)}, f32[1,576]{1,0:T(1,128)S(1)}, bf16[1,36,512]{2,1,0:T(8,128)(2,1)S(1)}) custom-call(s32[4,4]{1,0:T(4,128)} %mask_hbm.1, s32[4,4]{1,0:T(4,128)} %index_hbm.1, s32[1]{0:T(128)S(6)} %copy.11.fade_hbm, bf16[4,1,144,768]{3,2,1,0:T(8,128)(2,1)} %query_hbm.1, bf16[4,2,1,144,768]{4,3,2,1,0:T(8,128)(2,1)} %noisy_hbm.1, ...), custom_call_target="tpu_custom_call" | custom-call | tf_op jit(solution)/shard_map/pallas_call | solution.py:716
  30.4 1.1 %shard_map.105 = (bf16[4,1,144,768]{3,2,1,0:T(8,128)(2,1)}, bf16[1,36,512]{2,1,0:T(8,128)(2,1)}) custom-call(f32[4,1,144,768]{3,2,1,0:T(8,128)S(1)} %get-tuple-element.5.avg_ref, f32[1,576]{1,0:T(1,128)S(1)} %get-tuple-element.6.inv_ref, bf16[1,36,512]{2,1,0:T(8,128)(2,1)S(1)} %get-tuple-element.7.dec_ref), custom_call_target="tpu_custom_call" | custom-call | tf_op jit(solution)/shard_map/pallas_call | solution.py:780
